TPU v7x, 256 devices: a whole 4x4x8 slice. The times are simulated.
256 devices in a mesh: seq: 16 (over z_lo, x), mp: 16 (over y, z_hi, core).
Axes of the slice: x: 4, y: 4, z: 8 (z_hi: 2, z_lo: 4; z = z_hi * 4 + z_lo), core: 2. Of those that a mesh axis runs over, the one named last changes fastest.
Arguments:
- inputs: bfloat16 [8192, 7168], P('seq')
- norm_gain: float32 [7168], replicated, may hold values from 0.1 to 1.9
- qkv_weight: bfloat16 [7168, 3, 3584], P('seq', None, 'mp'), may hold values from -0.0625 to 0.0625
- adapter_down: bfloat16 [7168, 128], P('seq'), may hold values from -0.0625 to 0.0625
- adapter_up: bfloat16 [3, 128, 3584], P(None, None, 'mp'), may hold values from -0.5 to 0.5
- out_weight: bfloat16 [3584, 3584], P('mp', 'seq'), may hold values from -0.5 to 0.5
- cache_keys: bfloat16 [32, 256, 3584], P('seq', None, 'mp')
- cache_values: bfloat16 [32, 256, 3584], P('seq', None, 'mp'), may hold values from -6 to 6
- cache_lengths: int32 [4], replicated, may hold values from 1 to 2048, 5120 in all
- block_perm: int32 [32], replicated, may hold values from 0 to 31, each once
Outputs:
- block_out: bfloat16 [8192, 3584], P('seq', 'mp')
Inputs may be any that keep to these rules, and one draw needn't show every extreme that they name: `cache_lengths`: each request has at least one cached position, and some request fills all of its 8 blocks. `block_perm`: each logical block appears once.
All inputs are finite; a program needn't handle non-finite values.
Results may differ from a plain program's by a relative error of at most 0.025.
Values may be sent and summed in bfloat16 or wider, within the bound.
A program may use at most 192 MiB of HBM per device.

v0:
```python
import jax
import jax.numpy as jnp
from jax import lax
from jax.sharding import PartitionSpec as P

HD = 224
REQS = 4
QLEN = 2048
lowest = -1e30


def lookup(small_table, positions_of):
    hits = positions_of[..., None] == jnp.arange(small_table.shape[0], dtype=jnp.int32)
    return jnp.sum(jnp.where(hits, small_table, 0), axis=-1)


def query_meta(token_index, lengths):
    request = token_index // QLEN
    return (request, lookup(lengths, request) + token_index % QLEN)


def key_meta(row_index, layout, permutation, lengths):
    cache_rows, block_size, tok_dev, max_blocks = layout
    rows_dev = cache_rows + tok_dev
    device = row_index // rows_dev
    local_row = row_index % rows_dev
    block_index = (
        device * (cache_rows // block_size) + jnp.minimum(local_row, cache_rows - 1) // block_size
    )
    logical = lookup(permutation, block_index)
    request = logical // max_blocks
    position = logical % max_blocks * block_size + local_row % block_size
    cached_live = position < lookup(lengths, request)
    new_req, new_pos = query_meta(device * tok_dev + local_row - cache_rows, lengths)
    in_cache = local_row < cache_rows
    key_req = jnp.where(in_cache, jnp.where(cached_live, request, -1), new_req)
    return (key_req, jnp.where(in_cache, position, new_pos))


def attend(softmax_state, queries, query_info, key_rows, value_rows, key_info, head_dim):
    query_req, query_pos = query_info
    key_req, key_pos = key_info
    visible = (key_req[None, :] == query_req[:, None]) & (key_pos[None, :] <= query_pos[:, None])
    query_count = queries.shape[0]
    key_count = key_rows.shape[0]
    head_count = queries.shape[1] // head_dim
    summed, largest, weight_sum = softmax_state
    scores = jnp.einsum(
        "qhd,khd->hqk",
        queries.reshape(query_count, head_count, head_dim),
        key_rows.reshape(key_count, head_count, head_dim),
        preferred_element_type=jnp.float32,
    ) * head_dim ** (-0.5)
    scores = jnp.where(visible[None], scores, lowest)
    new_largest = jnp.maximum(largest, jnp.max(scores, axis=-1))
    weights = jnp.where(visible[None], jnp.exp(scores - new_largest[..., None]), 0.0)
    weight_sum = jnp.sum(weights, axis=-1)
    summed = jnp.einsum(
        "hqk,khd->hqd",
        weights.astype(jnp.bfloat16),
        value_rows.reshape(key_count, head_count, head_dim),
        preferred_element_type=jnp.float32,
    )
    return (summed, new_largest, weight_sum)


def per_device(
    inputs,
    norm_gain,
    qkv_weight,
    adapter_down,
    adapter_up,
    out_weight,
    cache_keys,
    cache_values,
    cache_lengths,
    block_perm,
):
    tok_dev = inputs.shape[0]
    widened = inputs.astype(jnp.float32)
    normed = (
        widened * lax.rsqrt(jnp.mean(widened * widened, axis=-1, keepdims=True) + 1e-05) * norm_gain
    ).astype(jnp.bfloat16)
    head_width = qkv_weight.shape[2]
    weight_rows = lax.all_gather(qkv_weight, "seq", axis=0, tiled=True)
    down_rows = lax.all_gather(adapter_down, "seq", axis=0, tiled=True)
    main_part = jnp.einsum("tr,rkc->ktc", normed, weight_rows, preferred_element_type=jnp.float32)
    low_rank = jnp.dot(normed, down_rows, preferred_element_type=jnp.float32)
    main_part, low_rank = (main_part, low_rank)
    low_rank = low_rank.astype(jnp.bfloat16)
    projected = (
        main_part
        + jnp.einsum("tr,krc->ktc", low_rank, adapter_up, preferred_element_type=jnp.float32)
    ).astype(jnp.bfloat16)
    queries = projected[0]
    new_keys = projected[1]
    new_values = projected[2]
    cycle_index = lax.axis_index("seq")
    cache_rows = cache_keys.shape[0] * cache_keys.shape[1]
    layout = (cache_rows, cache_keys.shape[1], tok_dev, block_perm.shape[0] // REQS)
    key_rows = jnp.concatenate([cache_keys.reshape(cache_rows, head_width), new_keys], axis=0)
    value_rows = jnp.concatenate([cache_values.reshape(cache_rows, head_width), new_values], axis=0)
    token_ids = jnp.arange(tok_dev, dtype=jnp.int32)
    own_info = query_meta(cycle_index * tok_dev + token_ids, cache_lengths)
    head_count = head_width // HD
    softmax_state = (
        jnp.zeros((head_count, tok_dev, HD), jnp.float32),
        jnp.full((head_count, tok_dev), lowest, jnp.float32),
        jnp.zeros((head_count, tok_dev), jnp.float32),
    )
    pieces = (
        lax.all_gather(key_rows, "seq", axis=0, tiled=True),
        lax.all_gather(value_rows, "seq", axis=0, tiled=True),
    )
    row_ids = jnp.arange(pieces[0].shape[0], dtype=jnp.int32)
    key_info = key_meta(row_ids, layout, block_perm, cache_lengths)
    softmax_state = attend(softmax_state, queries, own_info, pieces[0], pieces[1], key_info, HD)
    summed, largest, weight_sum = softmax_state
    attended = (
        (summed / weight_sum[..., None])
        .transpose(1, 0, 2)
        .reshape(tok_dev, head_width)
        .astype(jnp.bfloat16)
    )
    partial_value = jnp.dot(
        attended,
        lax.all_gather(out_weight, "seq", axis=1, tiled=True),
        preferred_element_type=jnp.float32,
    )
    return lax.psum_scatter(
        partial_value.astype(jnp.bfloat16), "mp", scatter_dimension=1, tiled=True
    )


def solution(mesh):
    in_specs = (
        P("seq", None),
        P(),
        P("seq", None, "mp"),
        P("seq", None),
        P(None, None, "mp"),
        P("mp", "seq"),
        P("seq", None, "mp"),
        P("seq", None, "mp"),
        P(),
        P(),
    )
    out_specs = P("seq", "mp")
    return jax.shard_map(
        per_device, mesh=mesh, in_specs=in_specs, out_specs=out_specs, check_vma=False
    )
```

profile of v0, /device:TPU:2, one launch (start us, length us, event | category | flops | bytes accessed | tf_op | source)
XLA Modules:
  0.0 670.6 jit_solution(3314007942279095606)
XLA Ops:
  6.5 0.7 all-gather.8.cloned.1.call-update
  7.3 2.6 copy.19
  10.0 1.0 copy.24
  11.0 4.6 fusion.5
  15.6 78.8 %all-gather.8.cloned.1.call-done = bf16[7168,128]{1,0:T(8,128)(2,1)} async-done(((bf16[448,128]{1,0:T(8,128)(2,1)}), bf16[7168,128]{1,0:T(8,128)(2,1)}) %all-gather.8.cloned.1.call-update) | async-done | bytes 1835024 | tf_op jit(solution)/shard_map/all_gather | solution.py:86
  94.4 6.3 fusion.16
  100.7 155.4 %all-gather.6.cloned.1.call-done = bf16[7168,3,224]{2,1,0:T(4,128)(2,1)} async-done(((bf16[448,3,224]{2,1,0:T(4,128)(2,1)}), bf16[7168,3,224]{2,1,0:T(4,128)(2,1)}) %all-gather.6.cloned.1.call-update) | async-done | bytes 9633808 | tf_op jit(solution)/shard_map/all_gather | solution.py:85
  256.0 21.6 %copy.20 = bf16[7168,3,224]{0,2,1:T(8,128)(2,1)} copy(bf16[7168,3,224]{2,1,0:T(4,128)(2,1)} %all-gather.6.cloned.1.call-done) | data formatting | bytes 19267584 | tf_op jit(solution)/shard_map/all_gather | solution.py:85
  277.7 10.2 %fusion.10 = f32[512,672]{0,1:S(1)} fusion(bf16[7168,672]{0,1:T(8,128)(2,1)} %bitcast.29, bf16[512,7168]{1,0:T(8,128)(2,1)} %param.10, f32[7168]{0:T(1024)S(1)} %copy-done.6, f32[512]{0:T(512)S(1)} %add_rsqrt_fusion), kind=kOutput, calls=%fused_computation.14 | convolution fusion | flops 4947181568 | bytes 18380800
  287.9 0.4 fusion.24
  288.3 0.8 pad_maximum_fusion
  289.2 0.8 pad_maximum_fusion.1
  290.1 0.8 copy.23
  290.9 0.2 reduce-scatter.2.cloned.1.call-start
  291.2 0.5 select_reduce_fusion
  291.9 0.4 select_reduce_fusion.2
  292.5 91.8 %all-gather.10.cloned.1.call-done = bf16[16384,224]{0,1:T(8,128)(2,1)} async-done(((bf16[1024,224]{0,1:T(8,128)(2,1)}), bf16[16384,224]{0,1:T(8,128)(2,1)}) %all-gather.10.cloned.1.call-update) | async-done | bytes 7340048 | tf_op jit(solution)/shard_map/all_gather | solution.py:112
  384.3 18.4 %fusion = (f32[512]{0:T(512)S(1)}, f32[512,16384]{1,0:T(8,128)}) fusion(s32[16384]{0:T(1024)S(1)} %get-tuple-element.10, s32[16384]{0:T(1024)S(1)} %get-tuple-element.9, s32[512]{0:T(512)S(1)} %fusion.49, s32[512]{0:T(512)S(1)} %add_select_fusion.9, bf16[16384,224]{0,1:T(8,128)(2,1)} %all-gather.10.cloned.1.call-done, bf16[3,512,224]{1,2,0:T(8,128)(2,1)S(1)} %fusion.24), kind=kOutput, calls=%fused_computation.3 | convolution fusion | flops 3808427520 | bytes 41261056 | tf_op jit(solution)/shard_map/qhd,khd->hqk/dot_general | solution.py:48
  402.7 16.7 %fusion.1 = f32[512]{0:T(512)S(1)} fusion(f32[512,16384]{1,0:T(8,128)} %get-tuple-element.12, f32[512]{0:T(512)S(1)} %broadcast_maximum_fusion, s32[16384]{0:T(1024)S(1)} %get-tuple-element.10, s32[16384]{0:T(1024)S(1)} %get-tuple-element.9, s32[512]{0:T(512)S(1)} %fusion.49, s32[512]{0:T(512)S(1)} %add_select_fusion.9), kind=kLoop, calls=%fused_computation.6 | loop fusion | flops 67108352 | bytes 33693696 | tf_op jit(solution)/shard_map/reduce_sum | solution.py:57
  419.4 59.4 %all-gather.12.cloned.1.call-done = bf16[16384,224]{0,1:T(8,128)(2,1)} async-done(((bf16[1024,224]{0,1:T(8,128)(2,1)}), bf16[16384,224]{0,1:T(8,128)(2,1)}) %all-gather.12.cloned.1.call-update) | async-done | bytes 7340048 | tf_op jit(solution)/shard_map/all_gather | solution.py:113
  478.7 17.6 %fusion.21 = bf16[512,224]{0,1:T(8,128)(2,1)S(1)} fusion(bf16[16384,224]{0,1:T(8,128)(2,1)} %all-gather.12.cloned.1.call-done, f32[512,16384]{1,0:T(8,128)} %get-tuple-element.12, f32[512]{0:T(512)S(1)} %broadcast_maximum_fusion, s32[16384]{0:T(1024)S(1)} %get-tuple-element.10, s32[16384]{0:T(1024)S(1)} %get-tuple-element.9, s32[512]{0:T(512)S(1)} %fusion.49, ...), kind=kOutput, calls=%fused_computation.21 | convolution fusion | flops 3825434624 | bytes 41263104 | tf_op jit(solution)/shard_map/hqk,khd->hqd/dot_general | solution.py:58
  496.3 64.7 %all-gather.14.cloned.1.call-done = bf16[224,3584]{0,1:T(8,128)(2,1)} async-done(((bf16[224,224]{0,1:T(8,128)(2,1)}), bf16[224,3584]{0,1:T(8,128)(2,1)}) %all-gather.14.cloned.1.call-update) | async-done | bytes 1605648 | tf_op jit(solution)/shard_map/all_gather | solution.py:127
  561.0 4.4 convolution_convert_fusion
  565.5 98.3 %reduce-scatter.2.cloned.1.call-done = bf16[512,224]{0,1:T(8,128)(2,1)} async-done(((bf16[512,3584]{0,1:T(8,128)(2,1)}), bf16[512,224]{0,1:T(8,128)(2,1)}) %reduce-scatter.2.cloned.1.call-update) | async-done | bytes 229392 | tf_op jit(solution)/shard_map/reduce_scatter | solution.py:130
  (34 shorter events, 0.7 us)
Async XLA Ops:
  6.5 87.8 %copy-start = (bf16[3,128,224]{1,2,0:T(8,128)(2,1)S(1)}, bf16[3,128,224]{1,2,0:T(8,128)(2,1)}, u32[]{:S(2)}) copy-start(bf16[3,128,224]{1,2,0:T(8,128)(2,1)} %param.14) | copy-start | bytes 516100
  6.5 87.8 %copy-start.6 = (f32[7168]{0:T(1024)S(1)}, f32[7168]{0:T(1024)}, u32[]{:S(2)}) copy-start(f32[7168]{0:T(1024)} %param.11) | copy-start | bytes 86020
  6.5 87.8 %all-gather.8.cloned.1.call-start = ((), (), s32[]{:S(2)}) async-start(), calls=%async_computation.2 | async-start | bytes 1949696 | tf_op jit(solution)/shard_map/all_gather | solution.py:86
  7.3 248.8 %all-gather.6.cloned.1.call-start = ((), (), s32[]{:S(2)}) async-start(), calls=%async_computation.1 | async-start | bytes 15597568 | tf_op jit(solution)/shard_map/all_gather | solution.py:85
  9.9 374.4 %all-gather.10.cloned.1.call-start = ((), (), s32[]{:S(2)}) async-start(), calls=%async_computation.3 | async-start | bytes 7798784 | tf_op jit(solution)/shard_map/all_gather | solution.py:112
  277.7 11.5 %copy-start.2 = (bf16[2,256,224]{1,2,0:T(8,128)(2,1)S(1)}, bf16[2,256,224]{1,2,0:T(8,128)(2,1)}, u32[]{:S(2)}) copy-start(bf16[2,256,224]{1,2,0:T(8,128)(2,1)} %param.17) | copy-start | bytes 688132
  277.7 12.4 %copy-start.3 = (bf16[224,224]{1,0:T(8,128)(2,1)S(1)}, bf16[224,224]{1,0:T(8,128)(2,1)}, u32[]{:S(2)}) copy-start(bf16[224,224]{1,0:T(8,128)(2,1)} %param.15) | copy-start | bytes 301060
  277.7 13.5 %copy-start.5 = (s32[32]{0:T(128)S(1)}, s32[32]{0:T(128)}, u32[]{:S(2)}) copy-start(s32[32]{0:T(128)} %param.19) | copy-start | bytes 388
  277.7 14.1 %copy-start.4 = (s32[4]{0:T(128)S(1)}, s32[4]{0:T(128)}, u32[]{:S(2)}) copy-start(s32[4]{0:T(128)} %param.18) | copy-start | bytes 52
  289.1 189.6 %all-gather.12.cloned.1.call-start = ((), (), s32[]{:S(2)}) async-start(), calls=%async_computation.4 | async-start | bytes 7798784 | tf_op jit(solution)/shard_map/all_gather | solution.py:113
  290.1 270.9 %all-gather.14.cloned.1.call-start = ((), (), s32[]{:S(2)}) async-start(), calls=%async_computation.5 | async-start | bytes 1949696 | tf_op jit(solution)/shard_map/all_gather | solution.py:127
  290.9 372.9 %reduce-scatter.2.cloned.1.call-start = ((), (), s32[]{:S(2)}) async-start(), calls=%async_computation.6 | async-start | bytes 3899392 | tf_op jit(solution)/shard_map/reduce_scatter | solution.py:130
  478.7 185.0 %copy-start.1 = (bf16[3,128,224]{1,2,0:T(8,128)(2,1)S(1)}, bf16[3,128,224]{1,2,0:T(8,128)(2,1)}, u32[]{:S(2)}) copy-start(bf16[3,128,224]{1,2,0:T(8,128)(2,1)} %param.14) | copy-start | bytes 516100
Sparse Core Ops, SparseCore 0:
  9.1 85.1 all-gather.7
  96.2 159.8 all-gather.5
  289.3 95.0 all-gather.9
  386.0 92.7 all-gather.11
  480.4 80.6 all-gather.13
  565.6 98.1 reduce-scatter.1
where the time goes:
time: 672 us; the launch traced here: 671 us
  waiting for transfers between devices  549 us (82%)
  matrix products  56.8 us (8%)
  local copies, waits for them, and re-layouts  26 us (4%)
  other arithmetic  24.6 us (4%)
  between operations  13.6 us (2%)
    all_gather x1, waiting for transfers between devices, per_device(): weight_rows = lax.all_gather(qkv_weight, 'seq', axis=0, tiled=True)  155 us
    reduce_scatter x1, waiting for transfers between devices, per_device(): lax.psum_scatter(partial_value.astype(jnp.bfloat16), 'mp', scatter_dimens...  98.3 us
    all_gather x1, waiting for transfers between devices, per_device(): lax.all_gather(key_rows, 'seq', axis=0, tiled=True)  91.8 us
    all_gather x1, waiting for transfers between devices, per_device(): down_rows = lax.all_gather(adapter_down, 'seq', axis=0, tiled=True)  78.8 us
    all_gather x1, waiting for transfers between devices, per_device(): lax.all_gather(out_weight, 'seq', axis=1, tiled=True)  64.7 us
    all_gather x1, waiting for transfers between devices, per_device(): lax.all_gather(value_rows, 'seq', axis=0, tiled=True)  59.4 us
    all_gather x1, local copies, waits for them, and re-layouts, per_device(): weight_rows = lax.all_gather(qkv_weight, 'seq', axis=0, tiled=True)  21.6 us
    dot_general x1, matrix products, attend(): jnp.einsum('qhd,khd->hqk', queries.reshape(query_count, head_count, head_...  18.4 us
  transfers between devices with their start and end apart: 6, of which 6 were waited for; matrix products, arithmetic and copies ran while one was open for 10% of the time, Pallas kernels for 0%

commit v1 on v0

--- a/solution.py
+++ b/solution.py
@@ -82,7 +82,16 @@
         widened * lax.rsqrt(jnp.mean(widened * widened, axis=-1, keepdims=True) + 1e-05) * norm_gain
     ).astype(jnp.bfloat16)
     head_width = qkv_weight.shape[2]
-    weight_rows = lax.all_gather(qkv_weight, "seq", axis=0, tiled=True)
+    replace_sides = lambda array_in: jnp.concatenate(
+        lax.all_to_all(
+            jnp.stack([array_in for _ in range(lax.axis_size("seq"))]),
+            axis_name="seq",
+            split_axis=0,
+            concat_axis=0,
+        ),
+        axis=0,
+    )
+    weight_rows = replace_sides(qkv_weight)
     down_rows = lax.all_gather(adapter_down, "seq", axis=0, tiled=True)
     main_part = jnp.einsum("tr,rkc->ktc", normed, weight_rows, preferred_element_type=jnp.float32)
     low_rank = jnp.dot(normed, down_rows, preferred_element_type=jnp.float32)

time: 672 us -> 725 us (1.079)
  local copies, waits for them, and re-layouts: 26 us -> 51.1 us
  waiting for transfers between devices: 549 us -> 569 us
  starting transfers between devices: 0.39 us -> 9.24 us
    all_gather x1 -> x0, waiting for transfers between devices: 155 us -> none  [per_device(): weight_rows = lax.all_gather(qkv_weight, 'seq', axis=0, tiled=True)]
    all_gather x1, waiting for transfers between devices: 78.8 us -> 210 us  [per_device(): down_rows = lax.all_gather(adapter_down, 'seq', axis=0, tiled=True)]
    all_gather x1, waiting for transfers between devices: 91.8 us -> 136 us  [per_device(): lax.all_gather(key_rows, 'seq', axis=0, tiled=True)]
    all_to_all x0 -> x1, local copies, waits for them, and re-layouts: none -> 25 us  [per_device(): lax.all_to_all(jnp.stack([array_in for _ in range(lax.axis_size('seq'))])...]
    all_gather x1 -> x0, local copies, waits for them, and re-layouts: 21.6 us -> none  [per_device(): weight_rows = lax.all_gather(qkv_weight, 'seq', axis=0, tiled=True)]
    unnamed x16 -> x19, local copies, waits for them, and re-layouts: 3.39 us -> 20.7 us
    all_to_all x0 -> x1, starting transfers between devices: none -> 9.04 us  [per_device(): lax.all_to_all(jnp.stack([array_in for _ in range(lax.axis_size('seq'))])...]
  transfers between devices with their start and end apart: 6 -> 6, of which waited for: 6 -> 5; matrix products, arithmetic and copies ran while one was open for 10% -> 9% of each run, Pallas kernels for 0% -> 0%
where the time goes in v1:
time: 725 us
  waiting for transfers between devices  569 us (78%)
  matrix products  56.8 us (8%)
  local copies, waits for them, and re-layouts  51.1 us (7%)
  other arithmetic  24.6 us (3%)
  between operations  13.3 us (2%)
  starting transfers between devices  9.24 us (1%)
    all_gather x1, waiting for transfers between devices, per_device(): down_rows = lax.all_gather(adapter_down, 'seq', axis=0, tiled=True)  210 us
    all_gather x1, waiting for transfers between devices, per_device(): lax.all_gather(key_rows, 'seq', axis=0, tiled=True)  136 us
    reduce_scatter x1, waiting for transfers between devices, per_device(): lax.psum_scatter(partial_value.astype(jnp.bfloat16), 'mp', scatter_dimens...  98.3 us
    all_gather x1, waiting for transfers between devices, per_device(): lax.all_gather(out_weight, 'seq', axis=1, tiled=True)  65 us
    all_gather x1, waiting for transfers between devices, per_device(): lax.all_gather(value_rows, 'seq', axis=0, tiled=True)  59.3 us
    all_to_all x1, local copies, waits for them, and re-layouts, per_device(): lax.all_to_all(jnp.stack([array_in for _ in range(lax.axis_size('seq'))])...  25 us
    unnamed x19, local copies, waits for them, and re-layouts  20.7 us
    dot_general x1, matrix products, attend(): jnp.einsum('qhd,khd->hqk', queries.reshape(query_count, head_count, head_...  18.4 us
  transfers between devices with their start and end apart: 6, of which 5 were waited for; matrix products, arithmetic and copies ran while one was open for 9% of the time, Pallas kernels for 0%

profile of v1, /device:TPU:2, one launch (start us, length us, event | category | flops | bytes accessed | tf_op | source)
XLA Modules:
  0.0 724.6 jit_solution(814809283104803685)
XLA Ops:
  6.5 1.4 copy.19
  7.9 5.3 stack.2
  13.3 9.0 %all-to-all-start = ((bf16[16,448,3,224]{1,3,2,0:T(8,128)(2,1)}), bf16[16,448,3,224]{1,3,2,0:T(8,128)(2,1)}, u32[]{:S(2)}, u32[]{:S(2)}) async-start(bf16[16,448,3,224]{1,3,2,0:T(8,128)(2,1)} %stack.2), calls=%async_computation | async-start | bytes 22020096 | tf_op jit(solution)/shard_map/all_to_all | solution.py:86
  22.4 0.7 all-gather.5.cloned.1.call-update
  23.1 4.6 fusion.5
  27.7 210.2 %all-gather.5.cloned.1.call-done = bf16[7168,128]{1,0:T(8,128)(2,1)} async-done(((bf16[448,128]{1,0:T(8,128)(2,1)}), bf16[7168,128]{1,0:T(8,128)(2,1)}) %all-gather.5.cloned.1.call-update) | async-done | bytes 1835024 | tf_op jit(solution)/shard_map/all_gather | solution.py:95
  238.0 6.3 fusion.16
  244.3 25.0 %copy.20 = bf16[16,448,3,224]{1,0,3,2:T(8,128)(2,1)} copy(bf16[16,448,3,224]{1,3,2,0:T(8,128)(2,1)} %all-to-all-done) | data formatting | bytes 19267584 | tf_op jit(solution)/shard_map/all_to_all | solution.py:86
  269.3 18.6 %reshape.274 = bf16[7168,672]{0,1:T(8,128)(2,1)} reshape(bf16[16,448,3,224]{1,0,3,2:T(8,128)(2,1)} %copy.20) | data formatting | bytes 19267584
  287.9 10.2 %fusion.10 = f32[512,672]{0,1:S(1)} fusion(bf16[7168,672]{0,1:T(8,128)(2,1)} %reshape.274, bf16[512,7168]{1,0:T(8,128)(2,1)} %param.10, f32[7168]{0:T(1024)S(1)} %copy-done.7, f32[512]{0:T(512)S(1)} %add_rsqrt_fusion), kind=kOutput, calls=%fused_computation.14 | convolution fusion | flops 4947181568 | bytes 18380800
  298.0 0.4 fusion.24
  298.5 0.8 pad_maximum_fusion
  299.4 0.8 pad_maximum_fusion.1
  300.3 0.8 copy.23
  301.2 0.5 select_reduce_fusion
  301.9 0.4 select_reduce_fusion.2
  302.5 135.9 %all-gather.7.cloned.1.call-done = bf16[16384,224]{0,1:T(8,128)(2,1)} async-done(((bf16[1024,224]{0,1:T(8,128)(2,1)}), bf16[16384,224]{0,1:T(8,128)(2,1)}) %all-gather.7.cloned.1.call-update) | async-done | bytes 7340048 | tf_op jit(solution)/shard_map/all_gather | solution.py:121
  438.3 18.4 %fusion = (f32[512]{0:T(512)S(1)}, f32[512,16384]{1,0:T(8,128)}) fusion(s32[16384]{0:T(1024)S(1)} %get-tuple-element.10, s32[16384]{0:T(1024)S(1)} %get-tuple-element.9, s32[512]{0:T(512)S(1)} %fusion.49, s32[512]{0:T(512)S(1)} %add_select_fusion.9, bf16[16384,224]{0,1:T(8,128)(2,1)} %all-gather.7.cloned.1.call-done, bf16[3,512,224]{1,2,0:T(8,128)(2,1)S(1)} %fusion.24), kind=kOutput, calls=%fused_computation.3 | convolution fusion | flops 3808427520 | bytes 41261056 | tf_op jit(solution)/shard_map/qhd,khd->hqk/dot_general | solution.py:48
  456.7 16.7 %fusion.1 = f32[512]{0:T(512)S(1)} fusion(f32[512,16384]{1,0:T(8,128)} %get-tuple-element.12, f32[512]{0:T(512)S(1)} %broadcast_maximum_fusion, s32[16384]{0:T(1024)S(1)} %get-tuple-element.10, s32[16384]{0:T(1024)S(1)} %get-tuple-element.9, s32[512]{0:T(512)S(1)} %fusion.49, s32[512]{0:T(512)S(1)} %add_select_fusion.9), kind=kLoop, calls=%fused_computation.6 | loop fusion | flops 67108352 | bytes 33693696 | tf_op jit(solution)/shard_map/reduce_sum | solution.py:57
  473.4 59.3 %all-gather.9.cloned.1.call-done = bf16[16384,224]{0,1:T(8,128)(2,1)} async-done(((bf16[1024,224]{0,1:T(8,128)(2,1)}), bf16[16384,224]{0,1:T(8,128)(2,1)}) %all-gather.9.cloned.1.call-update) | async-done | bytes 7340048 | tf_op jit(solution)/shard_map/all_gather | solution.py:122
  532.8 17.6 %fusion.21 = bf16[512,224]{0,1:T(8,128)(2,1)S(1)} fusion(bf16[16384,224]{0,1:T(8,128)(2,1)} %all-gather.9.cloned.1.call-done, f32[512,16384]{1,0:T(8,128)} %get-tuple-element.12, f32[512]{0:T(512)S(1)} %broadcast_maximum_fusion, s32[16384]{0:T(1024)S(1)} %get-tuple-element.10, s32[16384]{0:T(1024)S(1)} %get-tuple-element.9, s32[512]{0:T(512)S(1)} %fusion.49, ...), kind=kOutput, calls=%fused_computation.21 | convolution fusion | flops 3825434624 | bytes 41263104 | tf_op jit(solution)/shard_map/hqk,khd->hqd/dot_general | solution.py:58
  550.3 65.0 %all-gather.11.cloned.1.call-done = bf16[224,3584]{0,1:T(8,128)(2,1)} async-done(((bf16[224,224]{0,1:T(8,128)(2,1)}), bf16[224,3584]{0,1:T(8,128)(2,1)}) %all-gather.11.cloned.1.call-update) | async-done | bytes 1605648 | tf_op jit(solution)/shard_map/all_gather | solution.py:136
  615.3 4.4 convolution_convert_fusion
  619.7 98.3 %reduce-scatter.2.cloned.1.call-done = bf16[512,224]{0,1:T(8,128)(2,1)} async-done(((bf16[512,3584]{0,1:T(8,128)(2,1)}), bf16[512,224]{0,1:T(8,128)(2,1)}) %reduce-scatter.2.cloned.1.call-update) | async-done | bytes 229392 | tf_op jit(solution)/shard_map/reduce_scatter | solution.py:139
  (37 shorter events, 0.8 us)
Async XLA Ops:
  6.5 231.5 %copy-start = (bf16[3,128,224]{1,2,0:T(8,128)(2,1)S(1)}, bf16[3,128,224]{1,2,0:T(8,128)(2,1)}, u32[]{:S(2)}) copy-start(bf16[3,128,224]{1,2,0:T(8,128)(2,1)} %param.14) | copy-start | bytes 516100
  13.3 9.8 %copy-start.2 = (bf16[2,256,224]{1,2,0:T(8,128)(2,1)S(1)}, bf16[2,256,224]{1,2,0:T(8,128)(2,1)}, u32[]{:S(2)}) copy-start(bf16[2,256,224]{1,2,0:T(8,128)(2,1)} %param.16) | copy-start | bytes 688132
  13.3 224.7 %copy-start.7 = (f32[7168]{0:T(1024)S(1)}, f32[7168]{0:T(1024)}, u32[]{:S(2)}) copy-start(f32[7168]{0:T(1024)} %param.11) | copy-start | bytes 86020
  13.3 231.0 %all-to-all-start = ((bf16[16,448,3,224]{1,3,2,0:T(8,128)(2,1)}), bf16[16,448,3,224]{1,3,2,0:T(8,128)(2,1)}, u32[]{:S(2)}, u32[]{:S(2)}) async-start(bf16[16,448,3,224]{1,3,2,0:T(8,128)(2,1)} %stack.2), calls=%async_computation | async-start | bytes 22020096 | tf_op jit(solution)/shard_map/all_to_all | solution.py:86
  22.3 215.7 %all-gather.5.cloned.1.call-start = ((), (), s32[]{:S(2)}) async-start(), calls=%async_computation.2 | async-start | bytes 1949696 | tf_op jit(solution)/shard_map/all_gather | solution.py:95
  23.1 415.3 %all-gather.7.cloned.1.call-start = ((), (), s32[]{:S(2)}) async-start(), calls=%async_computation.3 | async-start | bytes 7798784 | tf_op jit(solution)/shard_map/all_gather | solution.py:121
  287.9 11.5 %copy-start.3 = (bf16[2,256,224]{1,2,0:T(8,128)(2,1)S(1)}, bf16[2,256,224]{1,2,0:T(8,128)(2,1)}, u32[]{:S(2)}) copy-start(bf16[2,256,224]{1,2,0:T(8,128)(2,1)} %param.17) | copy-start | bytes 688132
  287.9 12.5 %copy-start.4 = (bf16[224,224]{1,0:T(8,128)(2,1)S(1)}, bf16[224,224]{1,0:T(8,128)(2,1)}, u32[]{:S(2)}) copy-start(bf16[224,224]{1,0:T(8,128)(2,1)} %param.15) | copy-start | bytes 301060
  287.9 13.3 %copy-start.6 = (s32[32]{0:T(128)S(1)}, s32[32]{0:T(128)}, u32[]{:S(2)}) copy-start(s32[32]{0:T(128)} %param.19) | copy-start | bytes 388
  287.9 13.9 %copy-start.5 = (s32[4]{0:T(128)S(1)}, s32[4]{0:T(128)}, u32[]{:S(2)}) copy-start(s32[4]{0:T(128)} %param.18) | copy-start | bytes 52
  299.3 233.4 %all-gather.9.cloned.1.call-start = ((), (), s32[]{:S(2)}) async-start(), calls=%async_computation.4 | async-start | bytes 7798784 | tf_op jit(solution)/shard_map/all_gather | solution.py:122
  300.3 315.1 %all-gather.11.cloned.1.call-start = ((), (), s32[]{:S(2)}) async-start(), calls=%async_computation.5 | async-start | bytes 1949696 | tf_op jit(solution)/shard_map/all_gather | solution.py:136
  301.1 416.9 %reduce-scatter.2.cloned.1.call-start = ((), (), s32[]{:S(2)}) async-start(), calls=%async_computation.6 | async-start | bytes 3899392 | tf_op jit(solution)/shard_map/reduce_scatter | solution.py:139
  532.8 185.3 %copy-start.1 = (bf16[3,128,224]{1,2,0:T(8,128)(2,1)S(1)}, bf16[3,128,224]{1,2,0:T(8,128)(2,1)}, u32[]{:S(2)}) copy-start(bf16[3,128,224]{1,2,0:T(8,128)(2,1)} %param.14) | copy-start | bytes 516100
Sparse Core Ops, SparseCore 0:
  24.9 213.0 all-gather.4
  299.4 138.8 all-gather.6
  440.1 92.5 all-gather.8
  534.4 80.8 all-gather.10
  619.9 98.1 reduce-scatter.1
